TPU v7x, 512 devices: a whole 4x4x16 slice. The times are simulated.
512 devices in a mesh: group: 128 (over y_hi, z, x), tensor: 4 (over y_lo, core).
Axes of the slice: x: 4, y: 4 (y_hi: 2, y_lo: 2; y = y_hi * 2 + y_lo), z: 16, core: 2. Of those that a mesh axis runs over, the one named last changes fastest.
Arguments:
- block: bfloat16 [128, 128, 1024], P('group'), may hold values from -6 to 6
- mask: int32 [128, 128], P('group'), may hold values 0 or 1
- cache_len: int32 [128], replicated, may hold values from 128 to 1920, as said below
- cache_k: bfloat16 [128, 1024, 1024], P('group', None, 'tensor'), may hold values from -240 to 240
- cache_v: bfloat16 [128, 1024, 1024], P('group', None, 'tensor'), may hold values from -6 to 6
- w_q: bfloat16 [1024, 1024], P(None, 'tensor'), may hold values from -0.1875 to 0.1875
- b_q: bfloat16 [1024], P('tensor'), may hold values from -3 to 3
- w_k: bfloat16 [1024, 1024], P(None, 'tensor'), may hold values from -0.1875 to 0.1875
- b_k: bfloat16 [1024], P('tensor'), may hold values from -3 to 3
- w_v: bfloat16 [1024, 1024], P(None, 'tensor'), may hold values from -0.1875 to 0.1875
- b_v: bfloat16 [1024], P('tensor'), may hold values from -3 to 3
- w_o: bfloat16 [1024, 1024], P('tensor'), may hold values from -0.1875 to 0.1875
- b_o: bfloat16 [1024], replicated, may hold values from -3 to 3
- ln_gain: bfloat16 [1024], replicated, may hold values from 0.5 to 1.5
- ln_shift: bfloat16 [1024], replicated, may hold values from -3 to 3
Outputs:
- denoised: bfloat16 [128, 128, 1024], P('group')
Inputs may be any that keep to these rules, and one draw needn't show every extreme that they name: `cache_len`: in every pair exactly one request reads past its own group's slab into the partner's; the two lengths of a pair sum to at most 2048; both ends are reached in every draw.
All inputs are finite; a program needn't handle non-finite values. No bound on the sum of `mask` on one device may be relied on, other than what follows from the above.
Results may differ from a plain program's by a relative error of at most 0.03.
Values may be sent and summed in bfloat16 or wider, within the bound.
No kernel may reach another device: no remote copies, remote signals or barrier semaphores. Data moves between devices by JAX's collectives and lax.ppermute only.
A program may use at most 64 MiB of HBM per device.

v0:
```python
import jax
import jax.numpy as jnp
from jax import lax
from jax.sharding import PartitionSpec as P

HD = 64
NEG = -1e30
EPS = 1e-05


def swapped(array, axis, apart):
    return lax.ppermute(array, axis, [(i, i ^ 1 << apart) for i in range(lax.axis_size(axis))])


def project(inputs, weight, bias):
    return (
        jnp.dot(inputs, weight, preferred_element_type=jnp.float32) + bias.astype(jnp.float32)
    ).astype(jnp.bfloat16)


def layer_norm(summed, ln_gain, ln_shift):
    centre = summed - jnp.mean(summed, -1, keepdims=True)
    spread = jnp.mean(centre * centre, -1, keepdims=True)
    return (
        centre * lax.rsqrt(spread + EPS) * ln_gain.astype(jnp.float32)
        + ln_shift.astype(jnp.float32)
    ).astype(jnp.bfloat16)


def in_cache(length, req_parity, places, slab_len):
    return jnp.where(req_parity == 0, places < length, places >= 2 * slab_len - length)


def partial_attend(queries, keys, values, usable):
    row_count = queries.shape[0]
    head_count = queries.shape[1] // HD
    q_heads = queries.reshape(row_count, head_count, HD)
    k_heads = keys.reshape(keys.shape[0], head_count, HD)
    v_heads = values.reshape(values.shape[0], head_count, HD)
    scores = jnp.einsum(
        "qhd,khd->hqk", q_heads, k_heads, preferred_element_type=jnp.float32
    ) * HD ** (-0.5)
    scores = jnp.where(usable[None, None, :], scores, NEG)
    row_max = jnp.max(scores, -1)
    expo = jnp.exp(scores - row_max[:, :, None])
    row_sum = jnp.sum(expo, -1)
    summed_out = jnp.einsum(
        "hqk,khd->qhd", expo.astype(jnp.bfloat16), v_heads, preferred_element_type=jnp.float32
    )
    return (summed_out.reshape(row_count, head_count * HD), row_max, row_sum)


def body(
    block,
    mask,
    cache_len,
    cache_k,
    cache_v,
    w_q,
    b_q,
    w_k,
    b_k,
    w_v,
    b_v,
    w_o,
    b_o,
    ln_gain,
    ln_shift,
):
    tok_rows = block[0]
    own_k = cache_k[0]
    own_v = cache_v[0]
    slab_len = own_k.shape[0]
    group_idx = lax.axis_index("group")
    parity = group_idx % 2
    own_len = cache_len[group_idx]
    peer_k, peer_v = swapped((own_k, own_v), "group", 0)
    pool_k = jnp.where(
        parity == 0, jnp.concatenate([own_k, peer_k], 0), jnp.concatenate([peer_k, own_k], 0)
    )
    pool_v = jnp.where(
        parity == 0, jnp.concatenate([own_v, peer_v], 0), jnp.concatenate([peer_v, own_v], 0)
    )
    pool_usable = in_cache(own_len, parity, jnp.arange(2 * slab_len, dtype=jnp.int32), slab_len)

    def one_pass(inputs):
        queries = project(inputs, w_q, b_q)
        new_k = project(inputs, w_k, b_k)
        new_v = project(inputs, w_v, b_v)
        fresh = jnp.ones((inputs.shape[0],), bool)
        summed_out, row_max, row_sum = partial_attend(
            queries,
            jnp.concatenate([pool_k, new_k], 0),
            jnp.concatenate([pool_v, new_v], 0),
            jnp.concatenate([pool_usable, fresh], 0),
        )
        row_count = inputs.shape[0]
        head_count = row_sum.shape[0]
        attended = (
            (summed_out.reshape(row_count, head_count, HD) / row_sum.T[:, :, None])
            .reshape(row_count, head_count * HD)
            .astype(jnp.bfloat16)
        )
        partial_value = jnp.dot(attended, w_o, preferred_element_type=jnp.float32)
        summed = lax.psum(partial_value.astype(jnp.bfloat16), "tensor").astype(jnp.float32)
        return layer_norm(
            summed + b_o.astype(jnp.float32) + inputs.astype(jnp.float32), ln_gain, ln_shift
        )

    first_out = one_pass(tok_rows)
    second = jnp.where(mask[0][:, None] == 1, first_out, tok_rows)
    return one_pass(second)[None]


def solution(mesh):
    return jax.shard_map(
        body,
        mesh=mesh,
        in_specs=(
            P("group", None, None),
            P("group", None),
            P(),
            P("group", None, "tensor"),
            P("group", None, "tensor"),
            P(None, "tensor"),
            P("tensor"),
            P(None, "tensor"),
            P("tensor"),
            P(None, "tensor"),
            P("tensor"),
            P("tensor", None),
            P(),
            P(),
            P(),
        ),
        out_specs=P("group", None, None),
        check_vma=False,
    )
```

profile of v0, /device:TPU:1, one launch (start us, length us, event | category | flops | bytes accessed | tf_op | source)
XLA Modules:
  0.0 187.3 jit_solution(17652154022433314799)
XLA Ops:
  6.5 4.1 %collective-permute-start = (bf16[1024,256]{1,0:T(8,128)(2,1)}, bf16[1024,256]{1,0:T(8,128)(2,1)S(1)}, u32[]{:S(2)}, u32[]{:S(2)}) collective-permute-start(bf16[1024,256]{1,0:T(8,128)(2,1)} %bitcast.62), channel_id=1, source_target_pairs={{0,4},{4,0},{8,12},{12,8},{16,20},{20,16},{24,28},{28,24},{32,36},... | collective-permute-start | bytes 1572872 | tf_op jit(solution)/shard_map/ppermute | solution.py:12
  10.6 1.9 %collective-permute-start.1 = (bf16[1024,256]{1,0:T(8,128)(2,1)}, bf16[1024,256]{1,0:T(8,128)(2,1)}, u32[]{:S(2)}, u32[]{:S(2)}) collective-permute-start(bf16[1024,256]{1,0:T(8,128)(2,1)} %bitcast.64), channel_id=1, source_target_pairs={{0,4},{4,0},{8,12},{12,8},{16,20},{20,16},{24,28},{28,24},{32,36},... | collective-permute-start | bytes 1572872 | tf_op jit(solution)/shard_map/ppermute | solution.py:12
  13.2 1.2 dynamic_slice.3
  15.1 1.4 fusion.25
  18.6 1.4 fusion.26
  19.9 1.4 fusion.24
  22.1 6.7 %collective-permute-done.1 = bf16[1024,256]{1,0:T(8,128)(2,1)} collective-permute-done((bf16[1024,256]{1,0:T(8,128)(2,1)}, bf16[1024,256]{1,0:T(8,128)(2,1)}, u32[]{:S(2)}, u32[]{:S(2)}) %collective-permute-start.1) | collective-permute-done | bytes 524320 | tf_op jit(solution)/shard_map/ppermute | solution.py:12
  28.8 2.4 %maximum_select_fusion = (bf16[2048,256]{1,0:T(8,128)(2,1)S(1)}, bf16[2048,256]{1,0:T(8,128)(2,1)S(1)}) fusion(bf16[1024,256]{1,0:T(8,128)(2,1)} %copy-done.5, bf16[1024,256]{1,0:T(8,128)(2,1)S(1)} %bitcast.63, pred[]{:T(512)S(6)} %eq.21, bf16[1024,256]{1,0:T(8,128)(2,1)} %bitcast.65, bf16[1024,256]{1,0:T(8,128)(2,1)} %collective-permute-done.1), kind=kLoop, calls=%fused_computation.38 | loop fusion | flops 9437184 | bytes 4194305 | tf_op jit(solution)/shard_map/jit(_where)/select_n | solution.py:81
  31.2 1.1 pad_maximum_fusion.1
  32.3 2.3 %copy.24 = bf16[2176,256]{0,1:T(8,128)(2,1)} copy(bf16[2176,256]{1,0:T(8,128)(2,1)} %pad_maximum_fusion.1) | data formatting | bytes 2228224 | tf_op jit(solution)/shard_map/concatenate | solution.py:93
  34.6 1.1 pad_maximum_fusion
  35.7 2.3 %copy.22 = bf16[2176,256]{0,1:T(8,128)(2,1)} copy(bf16[2176,256]{1,0:T(8,128)(2,1)} %pad_maximum_fusion) | data formatting | bytes 2228224 | tf_op jit(solution)/shard_map/concatenate | solution.py:94
  38.0 2.1 %fusion.44 = (f32[4,128]{1,0:T(4,128)S(1)}, f32[4,128,2176]{2,1,0:T(8,128)S(1)}) fusion(bf16[128,4,64]{0,2,1:T(8,128)(2,1)S(1)} %bitcast.66, bf16[2176,4,64]{0,2,1:T(8,128)(2,1)} %bitcast.59, pred[2176]{0:T(1024)(128)(4,1)S(1)} %concatenate.31), kind=kOutput, calls=%fused_computation.61 | convolution fusion | flops 145948160 | bytes 5640320 | tf_op jit(solution)/shard_map/qhd,khd->hqk/dot_general | solution.py:40
  41.5 1.0 fusion.33
  42.5 1.0 convolution_convert_fusion.1
  43.6 62.3 %all-reduce.4.cloned.1.call-done = bf16[128,1024]{1,0:T(8,128)(2,1)} async-done(((bf16[128,1024]{1,0:T(8,128)(2,1)}), bf16[128,1024]{1,0:T(8,128)(2,1)}) %all-reduce.4.cloned.1.call-update) | async-done | bytes 262160 | tf_op jit(solution)/shard_map/psum | solution.py:105
  105.9 1.1 fusion.36
  107.1 1.2 multiply_reduce_fusion.1
  108.2 1.2 fusion.38
  109.4 1.3 fusion.29
  110.7 1.3 fusion.28
  112.0 1.3 fusion.27
  113.3 1.1 pad_maximum_fusion.3
  114.4 1.7 copy.27
  116.1 1.1 pad_maximum_fusion.2
  117.2 2.3 %copy.25 = bf16[2176,256]{0,1:T(8,128)(2,1)} copy(bf16[2176,256]{1,0:T(8,128)(2,1)} %pad_maximum_fusion.2) | data formatting | bytes 2228224 | tf_op jit(solution)/shard_map/concatenate | solution.py:94
  121.7 1.0 fusion.30
  122.7 1.0 convolution_convert_fusion
  123.7 52.7 %all-reduce.6.cloned.1.call-done = bf16[128,1024]{1,0:T(8,128)(2,1)} async-done(((bf16[128,1024]{1,0:T(8,128)(2,1)}), bf16[128,1024]{1,0:T(8,128)(2,1)}) %all-reduce.6.cloned.1.call-update) | async-done | bytes 262160 | tf_op jit(solution)/shard_map/psum | solution.py:105
  176.4 1.1 fusion.37
  177.5 1.2 multiply_reduce_fusion
  178.7 1.8 fusion.39
  (43 shorter events, 7.2 us)
Async XLA Ops:
  6.5 36.0 %copy-start = (bf16[256,1024]{1,0:T(8,128)(2,1)S(1)}, bf16[256,1024]{1,0:T(8,128)(2,1)}, u32[]{:S(2)}) copy-start(bf16[256,1024]{1,0:T(8,128)(2,1)} %param.26) | copy-start | bytes 1572868
  6.5 22.3 %copy-start.4 = (bf16[1,1024,256]{2,1,0:T(8,128)(2,1)S(1)}, bf16[1,1024,256]{2,1,0:T(8,128)(2,1)}, u32[]{:S(2)}) copy-start(bf16[1,1024,256]{2,1,0:T(8,128)(2,1)} %param.19) | copy-start | bytes 1572868
  6.5 99.4 %all-reduce.4.cloned.1.call-start = ((), (), s32[]{:S(2)}) async-start(), calls=%async_computation | async-start | bytes 524288 | tf_op jit(solution)/shard_map/psum | solution.py:105
  6.5 14.8 %collective-permute-start = (bf16[1024,256]{1,0:T(8,128)(2,1)}, bf16[1024,256]{1,0:T(8,128)(2,1)S(1)}, u32[]{:S(2)}, u32[]{:S(2)}) collective-permute-start(bf16[1024,256]{1,0:T(8,128)(2,1)} %bitcast.62), channel_id=1, source_target_pairs={{0,4},{4,0},{8,12},{12,8},{16,20},{20,16},{24,28},{28,24},{32,36},... | collective-permute-start | bytes 1572872 | tf_op jit(solution)/shard_map/ppermute | solution.py:12
  10.6 18.2 %collective-permute-start.1 = (bf16[1024,256]{1,0:T(8,128)(2,1)}, bf16[1024,256]{1,0:T(8,128)(2,1)}, u32[]{:S(2)}, u32[]{:S(2)}) collective-permute-start(bf16[1024,256]{1,0:T(8,128)(2,1)} %bitcast.64), channel_id=1, source_target_pairs={{0,4},{4,0},{8,12},{12,8},{16,20},{20,16},{24,28},{28,24},{32,36},... | collective-permute-start | bytes 1572872 | tf_op jit(solution)/shard_map/ppermute | solution.py:12
  21.3 0.8 copy-start.5
  40.2 1.3 copy-start.3
  41.4 2.1 %copy-start.6 = (bf16[1024]{0:T(1024)(128)(2,1)S(1)}, bf16[1024]{0:T(1024)(128)(2,1)}, u32[]{:S(2)}) copy-start(bf16[1024]{0:T(1024)(128)(2,1)} %param.27) | copy-start | bytes 6148
  41.4 2.1 %copy-start.7 = (bf16[1024]{0:T(1024)(128)(2,1)S(1)}, bf16[1024]{0:T(1024)(128)(2,1)}, u32[]{:S(2)}) copy-start(bf16[1024]{0:T(1024)(128)(2,1)} %param.28) | copy-start | bytes 6148
  41.4 2.1 %copy-start.8 = (bf16[1024]{0:T(1024)(128)(2,1)S(1)}, bf16[1024]{0:T(1024)(128)(2,1)}, u32[]{:S(2)}) copy-start(bf16[1024]{0:T(1024)(128)(2,1)} %param.29) | copy-start | bytes 6148
  41.4 2.2 %copy-start.9 = (s32[1,128]{1,0:T(1,128)S(1)}, s32[1,128]{1,0:T(1,128)}, u32[]{:S(2)}) copy-start(s32[1,128]{1,0:T(1,128)} %param.16) | copy-start | bytes 1540
  41.4 64.5 %copy-start.1 = (bf16[1,128,1024]{2,1,0:T(8,128)(2,1)S(1)}, bf16[1,128,1024]{2,1,0:T(8,128)(2,1)}, u32[]{:S(2)}) copy-start(bf16[1,128,1024]{2,1,0:T(8,128)(2,1)} %param.15) | copy-start | bytes 786436
  43.5 132.9 %all-reduce.6.cloned.1.call-start = ((), (), s32[]{:S(2)}) async-start(), calls=%async_computation.1 | async-start | bytes 524288 | tf_op jit(solution)/shard_map/psum | solution.py:105
  120.4 1.3 copy-start.2
Sparse Core Ops, SparseCore 0:
  43.6 62.2 all-reduce.3
  123.8 52.5 all-reduce.5
where the time goes:
time: 188 us; the launch traced here: 187 us
  waiting for transfers between devices  122 us (65%)
  other arithmetic  18.4 us (10%)
  matrix products  14.9 us (8%)
  between operations  14.3 us (8%)
  local copies, waits for them, and re-layouts  12 us (6%)
  starting transfers between devices  6.04 us (3%)
    psum x2, waiting for transfers between devices, one_pass(): lax.psum(partial_value.astype(jnp.bfloat16), 'tensor').astype(jnp.float32)  115 us
    dot_general x6, matrix products, project(): jnp.dot(inputs, weight, preferred_element_type=jnp.float32)  7.91 us
    ppermute x2, waiting for transfers between devices, swapped(): lax.ppermute(array, axis, [(i, i ^ 1 << apart) for i in range(lax.axis_si...  6.68 us
    ppermute x2, starting transfers between devices, swapped(): lax.ppermute(array, axis, [(i, i ^ 1 << apart) for i in range(lax.axis_si...  5.99 us
    concatenate x2, local copies, waits for them, and re-layouts, one_pass(): jnp.concatenate([pool_v, new_v], 0)  4.7 us
    concatenate x2, local copies, waits for them, and re-layouts, one_pass(): jnp.concatenate([pool_k, new_k], 0)  3.99 us
  transfers between devices with their start and end apart: 4, of which 3 were waited for; matrix products, arithmetic and copies ran while one was open for 4% of the time, Pallas kernels for 0%

commit v1 on v0

--- a/solution.py
+++ b/solution.py
@@ -102,7 +102,9 @@
             .astype(jnp.bfloat16)
         )
         partial_value = jnp.dot(attended, w_o, preferred_element_type=jnp.float32)
-        summed = lax.psum(partial_value.astype(jnp.bfloat16), "tensor").astype(jnp.float32)
+        summed = jnp.sum(
+            lax.all_gather(partial_value.astype(jnp.bfloat16), "tensor"), axis=0
+        ).astype(jnp.float32)
         return layer_norm(
             summed + b_o.astype(jnp.float32) + inputs.astype(jnp.float32), ln_gain, ln_shift
         )

time: 188 us -> 138 us (0.73)
  waiting for transfers between devices: 122 us -> 75.3 us
  other arithmetic: 18.4 us -> 15.9 us
  matrix products: 14.9 us -> 12.8 us
    psum x2 -> x0, waiting for transfers between devices: 115 us -> none  [one_pass(): lax.psum(partial_value.astype(jnp.bfloat16), 'tensor').astype(jnp.float32)]
    all_gather x0 -> x2, waiting for transfers between devices: none -> 68.6 us  [one_pass(): lax.all_gather(partial_value.astype(jnp.bfloat16), 'tensor')]
    reduce_sum x0 -> x2, other arithmetic: none -> 2.86 us  [one_pass(): jnp.sum(lax.all_gather(partial_value.astype(jnp.bfloat16), 'tensor'), axi...]
    dot_general x6, matrix products: 7.91 us -> 5.85 us  [project(): jnp.dot(inputs, weight, preferred_element_type=jnp.float32)]
    reduce_sum x2, other arithmetic: 2.23 us -> 0.34 us  [layer_norm(): centre = summed - jnp.mean(summed, -1, keepdims=True)]
    reduce_sum x2, other arithmetic: 2.3 us -> 0.42 us  [layer_norm(): spread = jnp.mean(centre * centre, -1, keepdims=True)]
  transfers between devices with their start and end apart: 4 -> 4, of which waited for: 3 -> 3; matrix products, arithmetic and copies ran while one was open for 4% -> 6% of each run, Pallas kernels for 0% -> 0%
where the time goes in v1:
time: 138 us; the launch traced here: 137 us
  waiting for transfers between devices  75.3 us (55%)
  other arithmetic  15.9 us (12%)
  between operations  14.5 us (11%)
  local copies, waits for them, and re-layouts  12.8 us (9%)
  matrix products  12.8 us (9%)
  starting transfers between devices  6.04 us (4%)
    all_gather x2, waiting for transfers between devices, one_pass(): lax.all_gather(partial_value.astype(jnp.bfloat16), 'tensor')  68.6 us
    ppermute x2, waiting for transfers between devices, swapped(): lax.ppermute(array, axis, [(i, i ^ 1 << apart) for i in range(lax.axis_si...  6.66 us
    ppermute x2, starting transfers between devices, swapped(): lax.ppermute(array, axis, [(i, i ^ 1 << apart) for i in range(lax.axis_si...  5.99 us
    dot_general x6, matrix products, project(): jnp.dot(inputs, weight, preferred_element_type=jnp.float32)  5.85 us
    concatenate x2, local copies, waits for them, and re-layouts, one_pass(): jnp.concatenate([pool_v, new_v], 0)  4.79 us
    concatenate x2, local copies, waits for them, and re-layouts, one_pass(): jnp.concatenate([pool_k, new_k], 0)  4.69 us
    dot_general x2, matrix products, partial_attend(): jnp.einsum('qhd,khd->hqk', q_heads, k_heads, preferred_element_type=jnp.f...  3 us
    reduce_sum x2, other arithmetic, one_pass(): jnp.sum(lax.all_gather(partial_value.astype(jnp.bfloat16), 'tensor'), axi...  2.86 us
  transfers between devices with their start and end apart: 4, of which 3 were waited for; matrix products, arithmetic and copies ran while one was open for 6% of the time, Pallas kernels for 0%

profile of v1, /device:TPU:1, one launch (start us, length us, event | category | flops | bytes accessed | tf_op | source)
XLA Modules:
  0.0 137.4 jit_solution(2170343801714944944)
XLA Ops:
  6.5 4.1 %collective-permute-start = (bf16[1024,256]{1,0:T(8,128)(2,1)}, bf16[1024,256]{1,0:T(8,128)(2,1)S(1)}, u32[]{:S(2)}, u32[]{:S(2)}) collective-permute-start(bf16[1024,256]{1,0:T(8,128)(2,1)} %bitcast.100), channel_id=1, source_target_pairs={{0,4},{4,0},{8,12},{12,8},{16,20},{20,16},{24,28},{28,24},{32,36},... | collective-permute-start | bytes 1572872 | tf_op jit(solution)/shard_map/ppermute | solution.py:12
  10.6 1.9 %collective-permute-start.1 = (bf16[1024,256]{1,0:T(8,128)(2,1)}, bf16[1024,256]{1,0:T(8,128)(2,1)}, u32[]{:S(2)}, u32[]{:S(2)}) collective-permute-start(bf16[1024,256]{1,0:T(8,128)(2,1)} %bitcast.102), channel_id=1, source_target_pairs={{0,4},{4,0},{8,12},{12,8},{16,20},{20,16},{24,28},{28,24},{32,36},... | collective-permute-start | bytes 1572872 | tf_op jit(solution)/shard_map/ppermute | solution.py:12
  13.2 1.2 dynamic_slice.3
  15.1 1.4 fusion.25
  17.9 0.7 convert_element_type.122
  18.6 1.4 fusion.26
  20.0 1.4 fusion.24
  21.4 0.8 copy-done.8
  22.1 6.7 %collective-permute-done.1 = bf16[1024,256]{1,0:T(8,128)(2,1)} collective-permute-done((bf16[1024,256]{1,0:T(8,128)(2,1)}, bf16[1024,256]{1,0:T(8,128)(2,1)}, u32[]{:S(2)}, u32[]{:S(2)}) %collective-permute-start.1) | collective-permute-done | bytes 524320 | tf_op jit(solution)/shard_map/ppermute | solution.py:12
  28.8 2.4 %maximum_select_fusion = (bf16[2048,256]{1,0:T(8,128)(2,1)S(1)}, bf16[2048,256]{1,0:T(8,128)(2,1)S(1)}) fusion(bf16[1024,256]{1,0:T(8,128)(2,1)} %copy-done.8, bf16[1024,256]{1,0:T(8,128)(2,1)S(1)} %bitcast.101, pred[]{:T(512)S(6)} %eq.21, bf16[1024,256]{1,0:T(8,128)(2,1)} %bitcast.103, bf16[1024,256]{1,0:T(8,128)(2,1)} %collective-permute-done.1), kind=kLoop, calls=%fused_computation.38 | loop fusion | flops 9437184 | bytes 4194305 | tf_op jit(solution)/shard_map/jit(_where)/select_n | solution.py:81
  31.2 1.1 pad_maximum_fusion.1
  32.3 2.3 %copy.24 = bf16[2176,256]{0,1:T(8,128)(2,1)} copy(bf16[2176,256]{1,0:T(8,128)(2,1)} %pad_maximum_fusion.1) | data formatting | bytes 2228224 | tf_op jit(solution)/shard_map/concatenate | solution.py:93
  34.7 1.1 pad_maximum_fusion
  35.7 2.4 %copy.22 = bf16[2176,256]{0,1:T(8,128)(2,1)} copy(bf16[2176,256]{1,0:T(8,128)(2,1)} %pad_maximum_fusion) | data formatting | bytes 2228224 | tf_op jit(solution)/shard_map/concatenate | solution.py:94
  38.1 2.1 %fusion.60 = (f32[4,128]{1,0:T(4,128)S(1)}, f32[4,128,2176]{2,1,0:T(8,128)S(1)}) fusion(bf16[128,4,64]{0,2,1:T(8,128)(2,1)S(1)} %bitcast.104, bf16[2176,4,64]{0,2,1:T(8,128)(2,1)} %bitcast.95, pred[2176]{0:T(1024)(128)(4,1)S(1)} %concatenate.31), kind=kOutput, calls=%fused_computation.78 | convolution fusion | flops 145948160 | bytes 5640320 | tf_op jit(solution)/shard_map/qhd,khd->hqk/dot_general | solution.py:40
  40.2 0.7 fusion.2
  41.5 1.0 fusion.33
  42.5 1.0 convolution_convert_fusion.1
  43.7 39.1 %all-gather.5.cloned.1.call-done = bf16[512,1024]{1,0:T(8,128)(2,1)} async-done(((bf16[128,1024]{1,0:T(8,128)(2,1)}), bf16[512,1024]{1,0:T(8,128)(2,1)}) %all-gather.5.cloned.1.call-update) | async-done | bytes 1048592 | tf_op jit(solution)/shard_map/all_gather | solution.py:106
  82.7 1.4 %reduce_sum.79 = bf16[128,1024]{1,0:T(8,128)(2,1)S(1)} reduce(bf16[4,128,1024]{2,1,0:T(8,128)(2,1)} %bitcast.98, bf16[]{:T(256)} %constant.43.clone.1), dimensions={0}, to_apply=%region_2.3 | reduce | flops 393216 | bytes 1310722 | tf_op jit(solution)/shard_map/reduce_sum | solution.py:105
  84.9 1.3 fusion.29
  86.8 1.1 pad_maximum_fusion.3
  87.9 2.3 %copy.27 = bf16[2176,256]{0,1:T(8,128)(2,1)} copy(bf16[2176,256]{1,0:T(8,128)(2,1)} %pad_maximum_fusion.3) | data formatting | bytes 2228224 | tf_op jit(solution)/shard_map/concatenate | solution.py:93
  90.3 1.1 pad_maximum_fusion.2
  91.4 2.4 %copy.25 = bf16[2176,256]{0,1:T(8,128)(2,1)} copy(bf16[2176,256]{1,0:T(8,128)(2,1)} %pad_maximum_fusion.2) | data formatting | bytes 2228224 | tf_op jit(solution)/shard_map/concatenate | solution.py:94
  93.9 0.9 fusion.61
  94.8 0.7 fusion.4
  96.0 1.0 fusion.30
  97.1 1.0 convolution_convert_fusion
  98.1 29.6 %all-gather.7.cloned.1.call-done = bf16[512,1024]{1,0:T(8,128)(2,1)} async-done(((bf16[128,1024]{1,0:T(8,128)(2,1)}), bf16[512,1024]{1,0:T(8,128)(2,1)}) %all-gather.7.cloned.1.call-update) | async-done | bytes 1048592 | tf_op jit(solution)/shard_map/all_gather | solution.py:106
  127.6 1.4 %reduce_sum.83 = bf16[128,1024]{1,0:T(8,128)(2,1)S(1)} reduce(bf16[4,128,1024]{2,1,0:T(8,128)(2,1)} %bitcast.99, bf16[]{:T(256)} %constant.43.clone.1), dimensions={0}, to_apply=%region_7.8 | reduce | flops 393216 | bytes 1310722 | tf_op jit(solution)/shard_map/reduce_sum | solution.py:105
  129.5 1.1 fusion.50
  (75 shorter events, 4.9 us)
Async XLA Ops:
  6.5 36.0 %copy-start = (bf16[256,1024]{1,0:T(8,128)(2,1)S(1)}, bf16[256,1024]{1,0:T(8,128)(2,1)}, u32[]{:S(2)}) copy-start(bf16[256,1024]{1,0:T(8,128)(2,1)} %param.26) | copy-start | bytes 1572868
  6.5 22.3 %copy-start.7 = (bf16[1,1024,256]{2,1,0:T(8,128)(2,1)S(1)}, bf16[1,1024,256]{2,1,0:T(8,128)(2,1)}, u32[]{:S(2)}) copy-start(bf16[1,1024,256]{2,1,0:T(8,128)(2,1)} %param.19) | copy-start | bytes 1572868
  6.5 76.2 %all-gather.5.cloned.1.call-start = ((), (), s32[]{:S(2)}) async-start(), calls=%async_computation | async-start | bytes 1310720 | tf_op jit(solution)/shard_map/all_gather | solution.py:106
  6.5 14.8 %collective-permute-start = (bf16[1024,256]{1,0:T(8,128)(2,1)}, bf16[1024,256]{1,0:T(8,128)(2,1)S(1)}, u32[]{:S(2)}, u32[]{:S(2)}) collective-permute-start(bf16[1024,256]{1,0:T(8,128)(2,1)} %bitcast.100), channel_id=1, source_target_pairs={{0,4},{4,0},{8,12},{12,8},{16,20},{20,16},{24,28},{28,24},{32,36},... | collective-permute-start | bytes 1572872 | tf_op jit(solution)/shard_map/ppermute | solution.py:12
  10.6 18.2 %collective-permute-start.1 = (bf16[1024,256]{1,0:T(8,128)(2,1)}, bf16[1024,256]{1,0:T(8,128)(2,1)}, u32[]{:S(2)}, u32[]{:S(2)}) collective-permute-start(bf16[1024,256]{1,0:T(8,128)(2,1)} %bitcast.102), channel_id=1, source_target_pairs={{0,4},{4,0},{8,12},{12,8},{16,20},{20,16},{24,28},{28,24},{32,36},... | collective-permute-start | bytes 1572872 | tf_op jit(solution)/shard_map/ppermute | solution.py:12
  13.2 8.1 %copy-start.11 = (f32[256]{0:T(256)}, f32[256]{0:T(256)S(1)}, u32[]{:S(2)}) copy-start(f32[256]{0:T(256)S(1)} %convert_element_type.124) | copy-start | bytes 3076
  17.8 13.4 %copy-start.15 = (f32[256]{0:T(256)}, f32[256]{0:T(256)S(1)}, u32[]{:S(2)}) copy-start(f32[256]{0:T(256)S(1)} %convert_element_type.126) | copy-start | bytes 3076
  18.6 12.6 %copy-start.13 = (f32[256]{0:T(256)}, f32[256]{0:T(256)S(1)}, u32[]{:S(2)}) copy-start(f32[256]{0:T(256)S(1)} %convert_element_type.122) | copy-start | bytes 3076
  21.3 0.8 copy-start.8
  40.2 1.3 copy-start.4
  41.5 2.1 %copy-start.17 = (bf16[1024]{0:T(1024)(128)(2,1)S(1)}, bf16[1024]{0:T(1024)(128)(2,1)}, u32[]{:S(2)}) copy-start(bf16[1024]{0:T(1024)(128)(2,1)} %param.27) | copy-start | bytes 6148
  41.5 2.1 %copy-start.18 = (bf16[1024]{0:T(1024)(128)(2,1)S(1)}, bf16[1024]{0:T(1024)(128)(2,1)}, u32[]{:S(2)}) copy-start(bf16[1024]{0:T(1024)(128)(2,1)} %param.28) | copy-start | bytes 6148
  41.5 2.1 %copy-start.19 = (bf16[1024]{0:T(1024)(128)(2,1)S(1)}, bf16[1024]{0:T(1024)(128)(2,1)}, u32[]{:S(2)}) copy-start(bf16[1024]{0:T(1024)(128)(2,1)} %param.29) | copy-start | bytes 6148
  41.5 2.2 %copy-start.24 = (s32[1,128]{1,0:T(1,128)S(1)}, s32[1,128]{1,0:T(1,128)}, u32[]{:S(2)}) copy-start(s32[1,128]{1,0:T(1,128)} %param.16) | copy-start | bytes 1540
  42.5 41.7 %copy-start.1 = (bf16[1,128,1024]{2,1,0:T(8,128)(2,1)S(1)}, bf16[1,128,1024]{2,1,0:T(8,128)(2,1)}, u32[]{:S(2)}) copy-start(bf16[1,128,1024]{2,1,0:T(8,128)(2,1)} %param.15) | copy-start | bytes 786436
  42.5 42.4 %copy-start.16 = (f32[256]{0:T(256)S(1)}, f32[256]{0:T(256)}, u32[]{:S(2)}) copy-start(f32[256]{0:T(256)} %copy-done.15) | copy-start | bytes 3076
  43.5 42.7 %copy-start.12 = (f32[256]{0:T(256)S(1)}, f32[256]{0:T(256)}, u32[]{:S(2)}) copy-start(f32[256]{0:T(256)} %copy-done.11) | copy-start | bytes 3076
  43.5 84.1 %all-gather.7.cloned.1.call-start = ((), (), s32[]{:S(2)}) async-start(), calls=%async_computation.1 | async-start | bytes 1310720 | tf_op jit(solution)/shard_map/all_gather | solution.py:106
  43.7 42.5 %copy-start.20 = (pred[128]{0:T(512)(128)(4,1)}, pred[128]{0:T(512)(128)(4,1)S(1)}, u32[]{:S(2)}) copy-start(pred[128]{0:T(512)(128)(4,1)S(1)} %compare_bitcast_fusion) | copy-start | bytes 388
  84.2 2.1 %copy-start.5 = (bf16[1024,256]{1,0:T(8,128)(2,1)S(1)}, bf16[1024,256]{1,0:T(8,128)(2,1)}, u32[]{:S(2)}) copy-start(bf16[1024,256]{1,0:T(8,128)(2,1)} %param.20) | copy-start | bytes 1572868
  84.2 2.3 %copy-start.6 = (bf16[1024,256]{1,0:T(8,128)(2,1)S(1)}, bf16[1024,256]{1,0:T(8,128)(2,1)}, u32[]{:S(2)}) copy-start(bf16[1024,256]{1,0:T(8,128)(2,1)} %param.24) | copy-start | bytes 1572868
  84.2 2.3 %copy-start.14 = (f32[256]{0:T(256)S(1)}, f32[256]{0:T(256)}, u32[]{:S(2)}) copy-start(f32[256]{0:T(256)} %copy-done.13) | copy-start | bytes 3076
  84.4 1.8 %copy-start.9 = (f32[128]{0:T(128)}, f32[128]{0:T(128)S(1)}, u32[]{:S(2)}) copy-start(f32[128]{0:T(128)S(1)} %broadcast_multiply_fusion.1) | copy-start | bytes 1540
  84.6 1.6 %copy-start.22 = (f32[128]{0:T(128)}, f32[128]{0:T(128)S(1)}, u32[]{:S(2)}) copy-start(f32[128]{0:T(128)S(1)} %add_rsqrt_fusion.1) | copy-start | bytes 1540
  91.4 2.4 %copy-start.2 = (bf16[2176,256]{0,1:T(8,128)(2,1)S(1)}, bf16[2176,256]{0,1:T(8,128)(2,1)}, u32[]{:S(2)}) copy-start(bf16[2176,256]{0,1:T(8,128)(2,1)} %copy.27) | copy-start | bytes 3342340
  94.7 1.3 copy-start.3
  97.0 32.4 %copy-start.10 = (f32[128]{0:T(128)S(1)}, f32[128]{0:T(128)}, u32[]{:S(2)}) copy-start(f32[128]{0:T(128)} %copy-done.9) | copy-start | bytes 1540
  97.1 32.4 %copy-start.21 = (pred[128]{0:T(512)(128)(4,1)S(1)}, pred[128]{0:T(512)(128)(4,1)}, u32[]{:S(2)}) copy-start(pred[128]{0:T(512)(128)(4,1)} %copy-done.20) | copy-start | bytes 388
  97.1 32.4 %copy-start.23 = (f32[128]{0:T(128)S(1)}, f32[128]{0:T(128)}, u32[]{:S(2)}) copy-start(f32[128]{0:T(128)} %copy-done.22) | copy-start | bytes 1540
Sparse Core Ops, SparseCore 0:
  43.6 39.0 all-gather.4
  98.2 29.3 all-gather.6
